TPU v7x, 32 devices: a whole 2x2x4 slice. The times are simulated.
32 devices in a mesh: grp: 4 (over x, core), seq: 8 (over z, y).
Axes of the slice: x: 2, y: 2, z: 4, core: 2. Of those that a mesh axis runs over, the one named last changes fastest.
Arguments:
- queries: bfloat16 [12288, 4096], P(('grp', 'seq')), may hold values from -6 to 6
- keys: bfloat16 [12288, 4096], P(('grp', 'seq')), may hold values from -6 to 6
- values: bfloat16 [12288, 4096], P(('grp', 'seq')), may hold values from -6 to 6
- gain: bfloat16 [4096], replicated, may hold values from 0.5 to 1.5
Outputs:
- attended: bfloat16 [12288, 4096], P(('grp', 'seq'))
All inputs are finite; a program needn't handle non-finite values.
Results may differ from a plain program's by a relative error of at most 0.0053.
Values sent between devices are 32-bit elements; how exact they have to be, the bound alone decides.
No kernel may reach another device: no remote copies, remote signals or barrier semaphores. Data moves between devices by JAX's collectives and lax.ppermute only.
A program may use at most 256 MiB of HBM per device.

v0:
```python
import jax
import jax.numpy as jnp
from jax import lax
from jax.sharding import PartitionSpec as P

HEADS = 32
HEAD_DIM = 128


def entering(value, axis, join, neutral):
    count, mine = (lax.axis_size(axis), lax.axis_index(axis))
    pieces = lax.all_gather(value, axis)
    subtotal = jnp.full_like(value, 0) + jnp.asarray(neutral, value.dtype)

    def lap(position, subtotal):
        longer = join(subtotal, pieces[position])
        return jnp.where(position < mine, longer, subtotal)

    return lax.fori_loop(0, count - 1, lap, subtotal)


def combine_sum(earlier, later):
    return earlier + later


def shards(queries, keys, values, gain):
    rows = queries.shape[0]
    fq = (
        jax.nn.silu(queries.astype(jnp.float32)).astype(jnp.bfloat16).reshape(rows, HEADS, HEAD_DIM)
    )
    fk = jax.nn.silu(keys.astype(jnp.float32)).astype(jnp.bfloat16).reshape(rows, HEADS, HEAD_DIM)
    vals = values.reshape(rows, HEADS, HEAD_DIM)
    local = jnp.einsum("thd,the->hde", fk, vals, preferred_element_type=jnp.float32)
    empty = jnp.zeros((HEADS, HEAD_DIM, HEAD_DIM), jnp.float32)
    within = entering(local, "seq", combine_sum, empty)
    total = lax.psum(local, "seq")
    before = entering(total, "grp", combine_sum, empty)
    carried = before + within
    positions = jnp.arange(rows, dtype=jnp.int32)
    causal = positions[:, None] >= positions[None, :]
    scores = jnp.einsum("thd,shd->hts", fq, fk, preferred_element_type=jnp.float32)
    scores = jnp.where(causal[None], scores, 0.0).astype(jnp.bfloat16)
    intra = jnp.einsum("hts,she->the", scores, vals, preferred_element_type=jnp.float32)
    inter = jnp.einsum(
        "thd,hde->the", fq, carried.astype(jnp.bfloat16), preferred_element_type=jnp.float32
    )
    mixed = intra + inter
    meansq = jnp.mean(mixed * mixed, axis=-1, keepdims=True)
    gains = gain.astype(jnp.float32).reshape(HEADS, HEAD_DIM)
    normed = mixed * lax.rsqrt(meansq + 1e-06) * gains[None]
    return normed.reshape(rows, HEADS * HEAD_DIM).astype(jnp.bfloat16)


def solution(mesh):
    return jax.shard_map(
        shards,
        mesh=mesh,
        in_specs=(P(("grp", "seq"), None), P(("grp", "seq"), None), P(("grp", "seq"), None), P()),
        out_specs=P(("grp", "seq"), None),
        check_vma=False,
    )
```

profile of v0, /device:TPU:0, one launch (start us, length us, event | category | flops | bytes accessed | tf_op | source)
XLA Modules:
  0.0 443.5 jit_solution(8854764190640074062)
XLA Ops:
  6.5 0.0 copy-start
  6.5 0.0 all-gather.6.cloned.1.call-start
  6.5 5.5 %fusion.10 = bf16[384,4096]{1,0:T(8,128)(2,1)} fusion(bf16[384,4096]{1,0:T(8,128)(2,1)} %param.9), kind=kLoop, calls=%fused_computation.17 | loop fusion | flops 9437184 | bytes 6291456 | tf_op jit(solution)/shard_map/convert_element_type | solution.py:31
  12.0 4.7 %copy.18 = bf16[384,4096]{0,1:T(8,128)(2,1)} copy(bf16[384,4096]{1,0:T(8,128)(2,1)} %fusion.10) | data formatting | bytes 6291456 | tf_op jit(solution)/shard_map/reshape | solution.py:31
  16.7 0.0 copy-done
  16.7 4.2 fusion.15
  20.9 0.0 copy-start.3
  20.9 0.0 all-gather.6.cloned.1.call-update
  21.0 230.2 %all-gather.6.cloned.1.call-done = f32[256,128,128]{2,1,0:T(8,128)} async-done(((f32[32,128,128]{2,1,0:T(8,128)}), f32[256,128,128]{2,1,0:T(8,128)}) %all-gather.6.cloned.1.call-update) | async-done | bytes 16777232 | tf_op jit(solution)/shard_map/all_gather | solution.py:12
  251.1 0.0 all-reduce.2.cloned.1.call-start
  251.1 0.7 all-reduce.2.cloned.1.call-update
  251.9 0.0 all-gather.4.cloned.1.call-start
  251.9 104.1 %all-reduce.2.cloned.1.call-done = f32[1,32,128,128]{3,2,1,0:T(8,128)} async-done(((f32[1,32,128,128]{3,2,1,0:T(8,128)}), f32[1,32,128,128]{3,2,1,0:T(8,128)}) %all-reduce.2.cloned.1.call-update) | async-done | bytes 2097168 | tf_op jit(solution)/shard_map/psum | solution.py:36
  356.0 0.0 all-gather.4.cloned.1.call-update
  356.1 0.0 copy-done.3
  356.2 9.2 %fusion = f32[32,384,128]{1,2,0:T(8,128)} fusion(pred[384,384]{1,0:T(8,128)(4,1)S(1)} %iota_compare_fusion, bf16[384,32,128]{0,2,1:T(8,128)(2,1)} %bitcast.58, bf16[384,4096]{1,0:T(8,128)(2,1)S(1)} %copy-done, bf16[384,4096]{1,0:T(8,128)(2,1)} %param.8), kind=kOutput, calls=%fused_computation.3 | convolution fusion | flops 2434793472 | bytes 15876096 | tf_op jit(solution)/shard_map/hts,she->the/dot_general | solution.py:43
  365.4 0.0 copy-start.2
  365.4 28.6 %while.29 = (s32[]{:T(128)}, f32[32,128,128]{2,1,0:T(8,128)}, s32[]{:T(128)}, f32[8,32,128,128]{3,2,1,0:T(8,128)}, s32[]{:T(128)}, /*index=5*/s32[]{:T(128)}) while((s32[]{:T(128)}, f32[32,128,128]{2,1,0:T(8,128)}, s32[]{:T(128)}, f32[8,32,128,128]{3,2,1,0:T(8,128)}, s32[]{:T(128)}, /*index=5*/s32[]{:T(128)}) %tuple.73), condition=%wide.region_4.5_spmd.clone, body=%wide.region_3.4_spmd.clone.sunk | while | flops 1572868 | bytes 6291557 | solution.py:19
  365.4 3.9 add_select_fusion.5
  369.3 4.2 add_select_fusion.5
  373.5 4.1 add_select_fusion.5
  377.6 4.1 add_select_fusion.5
  381.7 4.1 add_select_fusion.5
  385.7 4.2 add_select_fusion.5
  389.9 4.1 add_select_fusion.5
  394.0 21.2 %all-gather.4.cloned.1.call-done = f32[4,32,128,128]{3,2,1,0:T(8,128)} async-done(((f32[1,32,128,128]{3,2,1,0:T(8,128)}), f32[4,32,128,128]{3,2,1,0:T(8,128)}) %all-gather.4.cloned.1.call-update) | async-done | bytes 8388624 | tf_op jit(solution)/shard_map/all_gather | solution.py:12
  415.2 0.0 copy-done.2
  415.2 7.0 %while.28 = (s32[]{:T(128)}, f32[32,128,128]{2,1,0:T(8,128)S(1)}, s32[]{:T(128)}, f32[4,32,128,128]{3,2,1,0:T(8,128)}, s32[]{:T(128)}, /*index=5*/s32[]{:T(128)}) while((s32[]{:T(128)}, f32[32,128,128]{2,1,0:T(8,128)S(1)}, s32[]{:T(128)}, f32[4,32,128,128]{3,2,1,0:T(8,128)}, s32[]{:T(128)}, /*index=5*/s32[]{:T(128)}) %tuple.72), condition=%wide.region_2.3_spmd.clone, body=%wide.region_1.2_spmd.clone.sunk | while | flops 1572868 | bytes 6291557 | solution.py:19
  415.2 2.3 add_select_fusion.4
  417.5 2.3 add_select_fusion.4
  419.9 2.3 add_select_fusion.4
  422.2 0.0 slice-start
  422.2 0.0 slice-start.1
  422.2 7.4 %multiply_reduce_fusion = (f32[384,32]{0,1:T(8,128)S(1)}, f32[32,128,384]{2,1,0:T(8,128)S(1)}) fusion(f32[32,384,128]{1,2,0:T(8,128)} %fusion, f32[32,128,128]{2,1,0:T(8,128)S(1)} %get-tuple-element.163, f32[32,128,128]{2,1,0:T(8,128)} %get-tuple-element.164, bf16[384,4096]{1,0:T(8,128)(2,1)} %param.8), kind=kOutput, calls=%fused_computation.20 | convolution fusion | flops 417845248 | bytes 19972096 | tf_op jit(solution)/shard_map/thd,hde->the/dot_general | solution.py:44
  429.7 0.0 slice-done
  429.7 0.0 slice-done.1
  429.7 2.5 multiply_convert_fusion
  432.2 0.0 copy-start.1
  432.2 4.8 %copy.16 = bf16[384,4096]{1,0:T(8,128)(2,1)} copy(bf16[384,4096]{0,1:T(8,128)(2,1)} %bitcast.59) | data formatting | bytes 6291456 | tf_op jit(solution)/shard_map/convert_element_type | solution.py:51
  437.0 0.0 copy-done.1
  (6 shorter events, 0.1 us)
Async XLA Ops:
  6.5 10.2 %copy-start = (bf16[384,4096]{1,0:T(8,128)(2,1)S(1)}, bf16[384,4096]{1,0:T(8,128)(2,1)}, u32[]{:S(2)}) copy-start(bf16[384,4096]{1,0:T(8,128)(2,1)} %param.10) | copy-start | bytes 9437188
  6.5 244.6 %all-gather.6.cloned.1.call-start = ((), (), s32[]{:S(2)}) async-start(), calls=%async_computation.2 | async-start | bytes 18874368 | tf_op jit(solution)/shard_map/all_gather | solution.py:12
  20.9 335.2 %copy-start.3 = (bf16[4096]{0:T(1024)(128)(2,1)S(1)}, bf16[4096]{0:T(1024)(128)(2,1)}, u32[]{:S(2)}) copy-start(bf16[4096]{0:T(1024)(128)(2,1)} %param.11) | copy-start | bytes 24580
  251.1 104.9 %all-reduce.2.cloned.1.call-start = ((), (), s32[]{:S(2)}) async-start(), calls=%async_computation | async-start | bytes 4194304 | tf_op jit(solution)/shard_map/psum | solution.py:36
  251.9 163.3 %all-gather.4.cloned.1.call-start = ((), (), s32[]{:S(2)}) async-start(), calls=%async_computation.1 | async-start | bytes 10485760 | tf_op jit(solution)/shard_map/all_gather | solution.py:12
  365.4 49.8 %copy-start.2 = (f32[32,128,128]{2,1,0:T(8,128)S(1)}, f32[32,128,128]{2,1,0:T(8,128)}, u32[]{:S(2)}) copy-start(f32[32,128,128]{2,1,0:T(8,128)} %custom-call) | copy-start | bytes 6291460
  422.2 7.5 %slice-start = ((s8[6291456]{0:T(1024)(128)(4,1)}), s8[4194304]{0:T(1024)(128)(4,1)S(1)}, s32[]{:S(2)}) async-start(s8[6291456]{0:T(1024)(128)(4,1)} %bitcast.61), calls=%async_computation.3 | async-start | bytes 8388608
  422.2 7.5 %slice-start.1 = ((s8[6291456]{0:T(1024)(128)(4,1)}), s8[2097152]{0:T(1024)(128)(4,1)S(1)}, s32[]{:S(2)}) async-start(s8[6291456]{0:T(1024)(128)(4,1)} %bitcast.61), calls=%async_computation.4 | async-start | bytes 4194304
  432.2 4.8 %copy-start.1 = (bf16[384,4096]{1,0:T(8,128)(2,1)S(1)}, bf16[384,4096]{1,0:T(8,128)(2,1)}, u32[]{:S(2)}) copy-start(bf16[384,4096]{1,0:T(8,128)(2,1)} %param.10) | copy-start | bytes 9437188
Sparse Core Ops, SparseCore 0:
  21.1 229.9 all-gather.5
  255.6 100.4 all-reduce.1
  357.6 57.5 all-gather.3
where the time goes:
time: 444 us; the launch traced here: 443 us
  waiting for transfers between devices  356 us (80%)
  other arithmetic  43.6 us (10%)
  matrix products  20.9 us (5%)
  between operations  13.2 us (3%)
  local copies, waits for them, and re-layouts  9.5 us (2%)
    all_gather x2, waiting for transfers between devices, entering(): pieces = lax.all_gather(value, axis)  251 us
    psum x1, waiting for transfers between devices, shards(): total = lax.psum(local, 'seq')  104 us
    select_n x10, other arithmetic, lap(): return jnp.where(position < mine, longer, subtotal)  35.5 us
    dot_general x1, matrix products, shards(): jnp.einsum('hts,she->the', scores, vals, preferred_element_type=jnp.float32)  9.23 us
  transfers between devices with their start and end apart: 3, of which 3 were waited for; matrix products, arithmetic and copies ran while one was open for 9% of the time, Pallas kernels for 0%

commit v1 on v0

--- a/solution.py
+++ b/solution.py
@@ -33,7 +33,17 @@
     local = jnp.einsum("thd,the->hde", fk, vals, preferred_element_type=jnp.float32)
     empty = jnp.zeros((HEADS, HEAD_DIM, HEAD_DIM), jnp.float32)
     within = entering(local, "seq", combine_sum, empty)
-    total = lax.psum(local, "seq")
+
+    def use_digits(unit, along_axis="seq"):
+        nodes = lax.axis_size(along_axis)
+        val, u1 = (unit, 0)
+        while 1 << u1 < nodes:
+            s_next = lax.ppermute(val, along_axis, [(u, u ^ 1 << u1) for u in range(nodes)])
+            val = val + s_next
+            u1 = u1 + 1
+        return val
+
+    total = use_digits(local)
     before = entering(total, "grp", combine_sum, empty)
     carried = before + within
     positions = jnp.arange(rows, dtype=jnp.int32)

time: 444 us -> 539 us (1.21)
  waiting for transfers between devices: 356 us -> 447 us
  starting transfers between devices: 0.04 us -> 7.69 us
    ppermute x0 -> x3, waiting for transfers between devices: none -> 180 us  [use_digits(): lax.ppermute(val, along_axis, [(u, u ^ 1 << u1) for u in range(nodes)])]
    psum x1 -> x0, waiting for transfers between devices: 104 us -> none  [shards(): total = lax.psum(local, 'seq')]
    all_gather x2, waiting for transfers between devices: 251 us -> 266 us  [entering(): pieces = lax.all_gather(value, axis)]
    ppermute x0 -> x3, starting transfers between devices: none -> 7.47 us  [use_digits(): lax.ppermute(val, along_axis, [(u, u ^ 1 << u1) for u in range(nodes)])]
    select_n x10, other arithmetic: 35.5 us -> 28.3 us  [lap(): return jnp.where(position < mine, longer, subtotal)]
  transfers between devices with their start and end apart: 3 -> 5, of which waited for: 3 -> 5; matrix products, arithmetic and copies ran while one was open for 9% -> 4% of each run, Pallas kernels for 0% -> 0%
where the time goes in v1:
time: 539 us
  waiting for transfers between devices  447 us (83%)
  other arithmetic  40.1 us (7%)
  matrix products  20.8 us (4%)
  between operations  13.5 us (3%)
  local copies, waits for them, and re-layouts  9.48 us (2%)
  starting transfers between devices  7.69 us (1%)
    all_gather x2, waiting for transfers between devices, entering(): pieces = lax.all_gather(value, axis)  266 us
    ppermute x3, waiting for transfers between devices, use_digits(): lax.ppermute(val, along_axis, [(u, u ^ 1 << u1) for u in range(nodes)])  180 us
    select_n x10, other arithmetic, lap(): return jnp.where(position < mine, longer, subtotal)  28.3 us
  transfers between devices with their start and end apart: 5, of which 5 were waited for; matrix products, arithmetic and copies ran while one was open for 4% of the time, Pallas kernels for 0%

profile of v1, /device:TPU:0, one launch (start us, length us, event | category | flops | bytes accessed | tf_op | source)
XLA Modules:
  0.0 538.9 jit_solution(10502233655606403979)
XLA Ops:
  6.5 0.0 copy-start
  6.5 0.0 all-gather.5.cloned.1.call-start
  6.5 5.5 %fusion.10 = bf16[384,4096]{1,0:T(8,128)(2,1)} fusion(bf16[384,4096]{1,0:T(8,128)(2,1)} %param.9), kind=kLoop, calls=%fused_computation.17 | loop fusion | flops 9437184 | bytes 6291456 | tf_op jit(solution)/shard_map/convert_element_type | solution.py:31
  12.0 4.7 copy.18
  16.7 0.0 copy-done
  16.7 4.2 fusion.15
  20.9 3.0 collective-permute-start
  23.9 45.8 %collective-permute-done = f32[32,128,128]{2,1,0:T(8,128)S(1)} collective-permute-done((f32[32,128,128]{2,1,0:T(8,128)}, f32[32,128,128]{2,1,0:T(8,128)S(1)}, u32[]{:S(2)}, u32[]{:S(2)}) %collective-permute-start) | collective-permute-done | bytes 2097184 | tf_op jit(solution)/shard_map/ppermute | solution.py:41
  69.7 1.9 add.91
  71.6 1.9 collective-permute-start.1
  73.5 45.0 %collective-permute-done.1 = f32[32,128,128]{2,1,0:T(8,128)S(1)} collective-permute-done((f32[32,128,128]{2,1,0:T(8,128)S(1)}, f32[32,128,128]{2,1,0:T(8,128)S(1)}, u32[]{:S(2)}, u32[]{:S(2)}) %collective-permute-start.1) | collective-permute-done | bytes 2097184 | tf_op jit(solution)/shard_map/ppermute | solution.py:41
  118.5 0.3 add.92
  118.8 2.6 collective-permute-start.2
  121.4 89.2 %collective-permute-done.2 = f32[32,128,128]{2,1,0:T(8,128)S(1)} collective-permute-done((f32[32,128,128]{2,1,0:T(8,128)S(1)}, f32[32,128,128]{2,1,0:T(8,128)S(1)}, u32[]{:S(2)}, u32[]{:S(2)}) %collective-permute-start.2) | collective-permute-done | bytes 2097184 | tf_op jit(solution)/shard_map/ppermute | solution.py:41
  210.7 1.6 add.93
  212.2 0.0 copy-start.3
  212.2 0.0 all-gather.5.cloned.1.call-update
  212.2 0.2 all-gather.7.cloned.1.call-start
  212.5 0.5 all-gather.7.cloned.1.call-update
  213.1 0.0 copy-done.3
  213.1 9.2 %fusion = f32[32,384,128]{1,2,0:T(8,128)} fusion(pred[384,384]{1,0:T(8,128)(4,1)S(1)} %iota_compare_fusion, bf16[384,32,128]{0,2,1:T(8,128)(2,1)} %bitcast.58, bf16[384,4096]{1,0:T(8,128)(2,1)S(1)} %copy-done, bf16[384,4096]{1,0:T(8,128)(2,1)} %param.8), kind=kOutput, calls=%fused_computation.3 | convolution fusion | flops 2434793472 | bytes 15876096 | tf_op jit(solution)/shard_map/hts,she->the/dot_general | solution.py:53
  222.3 49.1 %all-gather.5.cloned.1.call-done = f32[128,128,128]{2,1,0:T(8,128)} async-done(((f32[32,128,128]{2,1,0:T(8,128)}), f32[128,128,128]{2,1,0:T(8,128)}) %all-gather.5.cloned.1.call-update) | async-done | bytes 8388624 | tf_op jit(solution)/shard_map/all_gather | solution.py:12
  271.5 0.0 copy-start.2
  271.5 12.1 %while.28 = (s32[]{:T(128)}, f32[32,128,128]{2,1,0:T(8,128)}, s32[]{:T(128)}, f32[4,32,128,128]{3,2,1,0:T(8,128)}, s32[]{:T(128)}, /*index=5*/s32[]{:T(128)}) while((s32[]{:T(128)}, f32[32,128,128]{2,1,0:T(8,128)}, s32[]{:T(128)}, f32[4,32,128,128]{3,2,1,0:T(8,128)}, s32[]{:T(128)}, /*index=5*/s32[]{:T(128)}) %tuple.71), condition=%wide.region_1.2_spmd.clone, body=%wide.region_0.1_spmd.clone.sunk | while | flops 1572868 | bytes 6291549 | solution.py:19
  271.5 3.6 add_select_fusion.4
  275.0 4.0 add_select_fusion.4
  279.1 4.5 add_select_fusion.4
  283.5 217.4 %all-gather.7.cloned.1.call-done = f32[256,128,128]{2,1,0:T(8,128)} async-done(((f32[32,128,128]{2,1,0:T(8,128)}), f32[256,128,128]{2,1,0:T(8,128)}) %all-gather.7.cloned.1.call-update) | async-done | bytes 16777232 | tf_op jit(solution)/shard_map/all_gather | solution.py:12
  500.9 0.0 copy-done.2
  500.9 16.3 %while.29 = (s32[]{:T(128)}, f32[32,128,128]{2,1,0:T(8,128)S(1)}, s32[]{:T(128)}, f32[8,32,128,128]{3,2,1,0:T(8,128)}, s32[]{:T(128)}, /*index=5*/s32[]{:T(128)}) while((s32[]{:T(128)}, f32[32,128,128]{2,1,0:T(8,128)S(1)}, s32[]{:T(128)}, f32[8,32,128,128]{3,2,1,0:T(8,128)}, s32[]{:T(128)}, /*index=5*/s32[]{:T(128)}) %tuple.72), condition=%wide.region_3.4_spmd.clone, body=%wide.region_2.3_spmd.clone.sunk | while | flops 1572868 | bytes 6291549 | solution.py:19
  500.9 2.3 add_select_fusion.5
  503.2 2.3 add_select_fusion.5
  505.6 2.3 add_select_fusion.5
  507.9 2.3 add_select_fusion.5
  510.2 2.3 add_select_fusion.5
  512.6 2.3 add_select_fusion.5
  514.9 2.3 add_select_fusion.5
  517.2 0.0 slice-start
  517.3 0.0 slice-start.1
  517.3 7.4 %multiply_reduce_fusion = (f32[384,32]{0,1:T(8,128)S(1)}, f32[32,128,384]{2,1,0:T(8,128)S(1)}) fusion(f32[32,384,128]{1,2,0:T(8,128)} %fusion, f32[32,128,128]{2,1,0:T(8,128)} %get-tuple-element.163, f32[32,128,128]{2,1,0:T(8,128)S(1)} %get-tuple-element.164, bf16[384,4096]{1,0:T(8,128)(2,1)} %param.8), kind=kOutput, calls=%fused_computation.20 | convolution fusion | flops 417845248 | bytes 19972096 | tf_op jit(solution)/shard_map/thd,hde->the/dot_general | solution.py:54
  524.7 0.0 slice-done
  524.7 0.0 slice-done.1
  524.8 2.5 multiply_convert_fusion
  527.2 0.0 copy-start.1
  527.2 4.8 copy.16
  532.0 0.0 copy-done.1
  (6 shorter events, 0.1 us)
Async XLA Ops:
  6.5 10.2 %copy-start = (bf16[384,4096]{1,0:T(8,128)(2,1)S(1)}, bf16[384,4096]{1,0:T(8,128)(2,1)}, u32[]{:S(2)}) copy-start(bf16[384,4096]{1,0:T(8,128)(2,1)} %param.10) | copy-start | bytes 9437188
  6.5 264.9 %all-gather.5.cloned.1.call-start = ((), (), s32[]{:S(2)}) async-start(), calls=%async_computation | async-start | bytes 10485760 | tf_op jit(solution)/shard_map/all_gather | solution.py:12
  20.9 48.8 %collective-permute-start = (f32[32,128,128]{2,1,0:T(8,128)}, f32[32,128,128]{2,1,0:T(8,128)S(1)}, u32[]{:S(2)}, u32[]{:S(2)}) collective-permute-start(f32[32,128,128]{2,1,0:T(8,128)} %fusion.15), channel_id=1, source_target_pairs={{0,1},{1,0},{2,3},{3,2},{4,5},{5,4},{6,7},{7,6},{8,9},{9,8},{10,11... | collective-permute-start | bytes 6291464 | tf_op jit(solution)/shard_map/ppermute | solution.py:41
  71.6 46.9 %collective-permute-start.1 = (f32[32,128,128]{2,1,0:T(8,128)S(1)}, f32[32,128,128]{2,1,0:T(8,128)S(1)}, u32[]{:S(2)}, u32[]{:S(2)}) collective-permute-start(f32[32,128,128]{2,1,0:T(8,128)S(1)} %add.91), channel_id=1, source_target_pairs={{0,2},{1,3},{2,0},{3,1},{4,6},{5,7},{6,4},{7,5},{8,10},{9,11},{10,... | collective-permute-start | bytes 6291464 | tf_op jit(solution)/shard_map/ppermute | solution.py:41
  118.8 91.8 %collective-permute-start.2 = (f32[32,128,128]{2,1,0:T(8,128)S(1)}, f32[32,128,128]{2,1,0:T(8,128)S(1)}, u32[]{:S(2)}, u32[]{:S(2)}) collective-permute-start(f32[32,128,128]{2,1,0:T(8,128)S(1)} %add.92), channel_id=1, source_target_pairs={{0,4},{1,5},{2,6},{3,7},{4,0},{5,1},{6,2},{7,3},{8,12},{9,13},{10,... | collective-permute-start | bytes 6291464 | tf_op jit(solution)/shard_map/ppermute | solution.py:41
  212.2 0.9 copy-start.3
  212.2 288.7 %all-gather.7.cloned.1.call-start = ((), (), s32[]{:S(2)}) async-start(), calls=%async_computation.1 | async-start | bytes 18874368 | tf_op jit(solution)/shard_map/all_gather | solution.py:12
  271.5 229.4 %copy-start.2 = (f32[32,128,128]{2,1,0:T(8,128)S(1)}, f32[32,128,128]{2,1,0:T(8,128)}, u32[]{:S(2)}) copy-start(f32[32,128,128]{2,1,0:T(8,128)} %custom-call.1) | copy-start | bytes 6291460
  517.2 7.5 %slice-start = ((s8[6291456]{0:T(1024)(128)(4,1)}), s8[4194304]{0:T(1024)(128)(4,1)S(1)}, s32[]{:S(2)}) async-start(s8[6291456]{0:T(1024)(128)(4,1)} %bitcast.61), calls=%async_computation.2 | async-start | bytes 8388608
  517.3 7.5 %slice-start.1 = ((s8[6291456]{0:T(1024)(128)(4,1)}), s8[2097152]{0:T(1024)(128)(4,1)S(1)}, s32[]{:S(2)}) async-start(s8[6291456]{0:T(1024)(128)(4,1)} %bitcast.61), calls=%async_computation.3 | async-start | bytes 4194304
  527.2 4.8 copy-start.1
Sparse Core Ops, SparseCore 0:
  212.4 59.0 all-gather.4
  273.6 227.2 all-gather.6
